TPU v7x, 128 devices: a whole 4x4x4 slice. The times are simulated.
128 devices in a mesh: leaf: 4 (over y_hi, core), front: 32 (over y_lo, z, x).
Axes of the slice: x: 4, y: 4 (y_hi: 2, y_lo: 2; y = y_hi * 2 + y_lo), z: 4, core: 2. Of those that a mesh axis runs over, the one named last changes fastest.
Arguments:
- leaf_source: float32 [4, 2048, 128], P('leaf', 'front'), may hold values from -6 to 6
- mid_source: float32 [4, 2048, 128], P('leaf', 'front'), may hold values from -6 to 6
- root_source: float32 [8192, 128], P('front'), may hold values from -6 to 6
- leaf_inverse: float32 [4, 2, 2048, 2048], P('leaf', None, 'front'), may hold values from -0.09375 to 0.09375
- leaf_coupling: float32 [4, 2, 4096, 2048], P('leaf', None, None, 'front'), may hold values from -0.09375 to 0.09375
- mid_inverse: float32 [4, 2, 2048, 4096], P('leaf', None, None, 'front'), may hold values from -0.0625 to 0.0625
- mid_coupling: float32 [4, 2, 8192, 2048], P('leaf', None, None, 'front'), may hold values from -0.0625 to 0.0625
- root_inverse: float32 [2, 8192, 8192], P(None, 'leaf', 'front'), may hold values from -0.046875 to 0.046875
- leaf_blocks: int32 [4, 32], P('leaf'), may hold values from 0 to 31, as said below
- mid_blocks: int32 [2, 64], replicated, may hold values from 0 to 63, as said below
Outputs:
- leaf_solution: float32 [4, 2048, 128], P('leaf', 'front')
- mid_solution: float32 [4, 2048, 128], P('leaf', 'front')
- root_solution: float32 [8192, 128], P('front')
Inputs may be any that keep to these rules, and one draw needn't show every extreme that they name: `leaf_blocks`: each row holds every block number of a level-1 separator exactly once. `mid_blocks`: each row holds every block number of the root separator exactly once.
All inputs are finite; a program needn't handle non-finite values.
Results may differ from a plain program's by a relative error of at most 0.00015.
Values sent between devices are 32-bit elements; how exact they have to be, the bound alone decides.
A program may use at most 128 MiB of HBM per device.

v0:
```python
import jax
import jax.numpy as jnp
from jax import lax
from jax.sharding import PartitionSpec as P

exact_precision = lax.Precision.HIGHEST


def partner(value, axis, apart):
    return lax.ppermute(value, axis, [(i, i ^ 1 << apart) for i in range(lax.axis_size(axis))])


def complex_apply(matrix, vectors):
    width = vectors.shape[1] // 2
    real_part = jnp.dot(
        matrix[0], vectors, precision=exact_precision, preferred_element_type=jnp.float32
    )
    imag_part = jnp.dot(
        matrix[1], vectors, precision=exact_precision, preferred_element_type=jnp.float32
    )
    return jnp.concatenate(
        [real_part[:, :width] - imag_part[:, width:], real_part[:, width:] + imag_part[:, :width]],
        axis=1,
    )


def complex_transposed(matrix, vectors):
    width = vectors.shape[1] // 2
    dims = (((0,), (0,)), ((), ()))
    real_part = lax.dot_general(
        matrix[0], vectors, dims, precision=exact_precision, preferred_element_type=jnp.float32
    )
    imag_part = lax.dot_general(
        matrix[1], vectors, dims, precision=exact_precision, preferred_element_type=jnp.float32
    )
    return jnp.concatenate(
        [real_part[:, :width] - imag_part[:, width:], real_part[:, width:] + imag_part[:, :width]],
        axis=1,
    )


def pick_rows(matrix, block_order, row_count):
    positions = jnp.arange(row_count, dtype=jnp.int32)
    sources = jnp.take(block_order, positions // 128) * 128 + positions % 128
    return jnp.take(matrix, sources, axis=1)


def gather_rows(local_rows, update, initial):
    return update(initial, lax.all_gather(local_rows, "front", axis=0, tiled=True), jnp.int32(0))


def scatter_rows(term, rows_each):
    return lax.psum_scatter(
        term(jnp.int32(0), rows_each * lax.axis_size("front")),
        "front",
        scatter_dimension=0,
        tiled=True,
    )


def pair_swap(values):
    return partner(values, "leaf", 0)


def group_total(values):
    return lax.psum(values, "leaf")


def body(
    leaf_source,
    mid_source,
    root_source,
    leaf_inverse,
    leaf_coupling,
    mid_inverse,
    mid_coupling,
    root_inverse,
    leaf_blocks,
    mid_blocks,
):
    front_count = lax.axis_size("front")
    group = lax.axis_index("leaf")
    side = group % 2
    source_two = leaf_source[0]
    inverse_two = leaf_inverse[0]
    coupling_two = leaf_coupling[0]
    inverse_one = mid_inverse[0]
    coupling_one = mid_coupling[0]
    order_two = jnp.argsort(leaf_blocks[0])
    order_one = jnp.argsort(lax.dynamic_index_in_dim(mid_blocks, group // 2, 0, keepdims=False))
    width2 = source_two.shape[1]
    rows_two = source_two.shape[0]
    half_rows = mid_source.shape[1]
    block_rows = coupling_two.shape[1] // front_count
    root_block = root_source.shape[0]

    def fold_inverse_two(carry, shard_piece, row_start):
        return complex_apply(inverse_two, shard_piece)

    solved_two = gather_rows(source_two, fold_inverse_two, jnp.zeros(source_two.shape, jnp.float32))

    def lift_two(row_start, row_count):
        return complex_apply(pick_rows(coupling_two, order_two, row_count), solved_two)

    lifted = scatter_rows(lift_two, block_rows)
    placed = lax.dynamic_update_slice_in_dim(
        jnp.zeros((block_rows, width2), jnp.float32), mid_source[0], side * half_rows, 0
    )
    own_part = placed - lifted
    reduced_one = own_part + pair_swap(own_part)

    def apply_one(row_start, row_count):
        return complex_apply(inverse_one, reduced_one)

    solved_one = scatter_rows(apply_one, half_rows)

    def lift_one(row_start, row_count):
        return complex_apply(pick_rows(coupling_one, order_one, row_count), solved_one)

    gathered_terms = group_total(scatter_rows(lift_one, root_block))
    reduced_root = root_source - gathered_terms

    def apply_root(row_start, row_count):
        return complex_apply(root_inverse, reduced_root)

    solved_root = scatter_rows(apply_root, root_inverse.shape[1] // front_count)

    def fold_root(carry, shard_piece, row_start):
        return complex_transposed(root_inverse, shard_piece)

    partial_root = gather_rows(solved_root, fold_root, jnp.zeros(root_source.shape, jnp.float32))
    root_solution = group_total(partial_root)

    def fold_mid(carry, shard_piece, row_start):
        return complex_transposed(
            pick_rows(coupling_one, order_one, shard_piece.shape[0]), shard_piece
        )

    pulled_one = gather_rows(root_solution, fold_mid, jnp.zeros(solved_one.shape, jnp.float32))
    rest_one = solved_one - pulled_one

    def fold_inverse_one(carry, shard_piece, row_start):
        return complex_transposed(inverse_one, shard_piece)

    own_columns = gather_rows(
        rest_one, fold_inverse_one, jnp.zeros((block_rows, width2), jnp.float32)
    )
    mid_block = own_columns + pair_swap(own_columns)
    mid_solution = lax.dynamic_slice_in_dim(mid_block, side * half_rows, half_rows, 0)

    def fold_leaf(carry, shard_piece, row_start):
        return complex_transposed(
            pick_rows(coupling_two, order_two, shard_piece.shape[0]), shard_piece
        )

    pulled_two = gather_rows(mid_block, fold_leaf, jnp.zeros(solved_two.shape, jnp.float32))
    rest_two = solved_two - pulled_two

    def apply_leaf_back(row_start, row_count):
        return complex_transposed(inverse_two, rest_two)

    leaf_solution = scatter_rows(apply_leaf_back, rows_two)
    return (leaf_solution[None], mid_solution[None], root_solution)


def solution(mesh):
    placed = (
        P("leaf", "front", None),
        P("leaf", "front", None),
        P("front", None),
        P("leaf", None, "front", None),
        P("leaf", None, None, "front"),
        P("leaf", None, None, "front"),
        P("leaf", None, None, "front"),
        P(None, "leaf", "front"),
        P("leaf", None),
        P(),
    )
    return jax.shard_map(
        body,
        mesh=mesh,
        in_specs=placed,
        out_specs=(P("leaf", "front", None), P("leaf", "front", None), P("front", None)),
        check_vma=False,
    )
```

profile of v0, /device:TPU:0, one launch (start us, length us, event | category | flops | bytes accessed | tf_op | source)
XLA Modules:
  0.0 1807.4 jit_solution(7411422771738973150)
XLA Ops:
  8.0 2.3 sort.34
  11.7 6.2 copy.32
  17.8 19.9 %broadcast_clamp_fusion.1 = s32[4096]{0:T(1024)S(1)} fusion(s32[]{:T(128)} %bitcast.35, s32[]{:T(128)} %bitcast.34, s32[]{:T(128)} %bitcast.33, s32[]{:T(128)} %bitcast.32, s32[]{:T(128)} %bitcast.31, s32[]{:T(128)} %bitcast.30, s32[]{:T(128)} %bitcast.29, s32[]{:T(128)} %bitcast.28, s32[]{:T(128)} %bitcast.27, s32[]{:T(128)} %bitcast.26, s32[]{:T(128)} %bitcast.25, ...), kind=kLoop, calls=%fused_computation.211 | loop fusion | flops 356352 | bytes 16512 | tf_op gather
  37.7 30.5 %gather_fusion = f32[4096,2,64]{2,1,0:T(2,128)} fusion(f32[2,4096,64]{2,0,1:T(2,128)} %bitcast.203, s32[4096]{0:T(1024)S(1)} %broadcast_clamp_fusion.1), kind=kCustom, calls=%fused_computation.clone | custom fusion | bytes 4210688 | tf_op jit(solution)/shard_map/jit(_take)/gather | solution.py:45
  68.3 19.9 %compare_and_fusion.1 = pred[4096]{0:T(1024)(128)(4,1)S(1)} fusion(s32[]{:T(128)} %bitcast.35, s32[]{:T(128)} %bitcast.34, s32[]{:T(128)} %bitcast.33, s32[]{:T(128)} %bitcast.32, s32[]{:T(128)} %bitcast.31, s32[]{:T(128)} %bitcast.30, s32[]{:T(128)} %bitcast.29, s32[]{:T(128)} %bitcast.28, s32[]{:T(128)} %bitcast.27, s32[]{:T(128)} %bitcast.26, ...), kind=kLoop, calls=%fused_computation.210 | loop fusion | flops 364544 | bytes 4224 | tf_op jit(solution)/shard_map/jit(_take)/and | solution.py:45
  88.2 16.3 select_bitcast_fusion.1
  104.5 4.1 fusion.158
  108.6 54.6 %all-gather.15.cloned.1.call-done = f32[1,2048,128]{2,1,0:T(8,128)} async-done(((f32[1,64,128]{2,1,0:T(8,128)}), f32[1,2048,128]{2,1,0:T(8,128)}) %all-gather.15.cloned.1.call-update) | async-done | bytes 1048592 | tf_op jit(solution)/shard_map/all_gather | solution.py:49
  163.2 2.1 fusion.20
  165.4 2.0 fusion.22
  167.5 2.1 fusion.165
  169.6 2.1 fusion.166
  172.1 1.5 pad_maximum_fusion.1
  173.8 2.0 sort.35
  179.1 39.6 %compare_and_fusion = (pred[8192]{0:T(1024)(128)(4,1)S(1)}, s32[8192]{0:T(1024)S(1)}) fusion(s32[]{:T(128)} %bitcast.109, s32[]{:T(128)} %bitcast.108, s32[]{:T(128)} %bitcast.107, s32[]{:T(128)} %bitcast.106, s32[]{:T(128)} %bitcast.105, s32[]{:T(128)} %bitcast.104, s32[]{:T(128)} %bitcast.103, s32[]{:T(128)} %bitcast.102, s32[]{:T(128)} %bitcast.101, ...), kind=kLoop, calls=%fused_computation.166 | loop fusion | flops 1253376 | bytes 41216 | tf_op jit(solution)/shard_map/jit(_take)/and | solution.py:45
  218.7 118.7 %reduce-scatter.12.cloned.1.call-done = f32[128,128]{0,1:T(8,128)} async-done(((f32[4096,128]{0,1:T(8,128)}), f32[128,128]{0,1:T(8,128)}) %reduce-scatter.12.cloned.1.call-update) | async-done | bytes 65552 | tf_op jit(solution)/shard_map/reduce_scatter | solution.py:53
  338.5 10.8 copy.34
  349.3 59.6 %gather_fusion.1 = f32[8192,2,64]{2,1,0:T(2,128)} fusion(f32[2,8192,64]{2,0,1:T(2,128)} %bitcast.198, s32[8192]{0:T(1024)S(1)} %broadcast_clamp_fusion), kind=kCustom, calls=%fused_computation.1.clone | custom fusion | bytes 8421376 | tf_op jit(solution)/shard_map/jit(_take)/gather | solution.py:45
  408.9 2.2 convolution_bitcast_fusion.3
  411.1 2.2 convolution_bitcast_fusion.2
  414.6 2.6 copy.41
  417.3 29.5 %select_bitcast_fusion = f32[2,8192,64]{2,0,1:T(2,128)S(1)} fusion(f32[8192,2,64]{2,1,0:T(2,128)} %gather_fusion.1, pred[8192]{0:T(1024)(128)(4,1)S(1)} %get-tuple-element.20), kind=kLoop, calls=%fused_computation.2 | loop fusion | flops 1048576 | bytes 8396800 | tf_op jit(solution)/shard_map/jit(_take)/select_n | solution.py:45
  446.8 7.7 fusion.157
  454.5 120.2 %reduce-scatter.16.cloned.1.call-done = f32[64,128]{1,0:T(8,128)} async-done(((f32[2048,128]{1,0:T(8,128)}), f32[64,128]{1,0:T(8,128)}) %reduce-scatter.16.cloned.1.call-update) | async-done | bytes 32784
  574.7 6.0 fusion.167
  580.8 4.4 fusion.168
  585.7 2.3 pad_maximum_fusion
  588.1 165.2 %reduce-scatter.14.cloned.1.call-done = f32[256,128]{0,1:T(8,128)} async-done(((f32[8192,128]{0,1:T(8,128)}), f32[256,128]{0,1:T(8,128)}) %reduce-scatter.14.cloned.1.call-update) | async-done | bytes 131088 | tf_op jit(solution)/shard_map/reduce_scatter | solution.py:53
  753.9 38.4 %all-reduce.3.cloned.1.call-done = f32[256,128]{0,1:T(8,128)} async-done(((f32[256,128]{0,1:T(8,128)}), f32[256,128]{0,1:T(8,128)}) %all-reduce.3.cloned.1.call-update) | async-done | bytes 131088 | tf_op jit(solution)/shard_map/psum | solution.py:66
  792.3 3.9 convolution_bitcast_fusion.5
  796.2 3.9 convolution_bitcast_fusion.4
  801.3 2.6 copy.43
  803.9 160.8 %reduce-scatter.18.cloned.1.call-done = f32[64,128]{1,0:T(8,128)} async-done(((f32[2048,128]{1,0:T(8,128)}), f32[64,128]{1,0:T(8,128)}) %reduce-scatter.18.cloned.1.call-update) | async-done | bytes 32784 | tf_op jit(solution)/shard_map/reduce_scatter | solution.py:53
  964.8 148.6 %all-gather.7.cloned.1.call-done = f32[2048,128]{1,0:T(8,128)} async-done(((f32[64,128]{1,0:T(8,128)}), f32[2048,128]{1,0:T(8,128)}) %all-gather.7.cloned.1.call-update) | async-done | bytes 1048592 | tf_op jit(solution)/shard_map/all_gather | solution.py:49
  1113.4 3.8 fusion.10
  1117.2 3.8 fusion.13
  1121.7 40.5 %all-reduce.5.cloned.1.call-done = f32[256,128]{0,1:T(8,128)} async-done(((f32[256,128]{0,1:T(8,128)}), f32[256,128]{0,1:T(8,128)}) %all-reduce.5.cloned.1.call-update) | async-done | bytes 131088 | tf_op jit(solution)/shard_map/psum | solution.py:66
  1162.4 158.7 %all-gather.9.cloned.1.call-done = f32[8192,128]{0,1:T(8,128)} async-done(((f32[256,128]{0,1:T(8,128)}), f32[8192,128]{0,1:T(8,128)}) %all-gather.9.cloned.1.call-update) | async-done | bytes 4194320 | tf_op jit(solution)/shard_map/all_gather | solution.py:49
  1321.1 10.3 fusion.169
  1331.5 7.1 fusion.170
  1339.4 150.8 %all-gather.11.cloned.1.call-done = f32[2048,128]{1,0:T(8,128)} async-done(((f32[64,128]{1,0:T(8,128)}), f32[2048,128]{1,0:T(8,128)}) %all-gather.11.cloned.1.call-update) | async-done | bytes 1048592 | tf_op jit(solution)/shard_map/all_gather | solution.py:49
  1490.3 3.4 convolution_bitcast_fusion.6
  1493.6 3.4 convolution_bitcast_fusion.7
  1499.0 125.6 %all-gather.13.cloned.1.call-done = f32[4096,128]{0,1:T(8,128)} async-done(((f32[128,128]{0,1:T(8,128)}), f32[4096,128]{0,1:T(8,128)}) %all-gather.13.cloned.1.call-update) | async-done | bytes 2097168 | tf_op jit(solution)/shard_map/all_gather | solution.py:49
  1624.6 5.8 fusion.171
  1630.5 3.5 fusion.172
  1636.6 1.3 copy.45
  1639.5 159.1 %reduce-scatter.20.cloned.1.call-done = f32[64,128]{1,0:T(8,128)} async-done(((f32[2048,128]{1,0:T(8,128)}), f32[64,128]{1,0:T(8,128)}) %reduce-scatter.20.cloned.1.call-update) | async-done | bytes 32784
  (94 shorter events, 20.3 us)
Async XLA Ops:
  7.2 166.6 %copy-start = (s32[2,64]{1,0:T(2,128)S(1)}, s32[2,64]{1,0:T(2,128)}, u32[]{:S(2)}) copy-start(s32[2,64]{1,0:T(2,128)} %param.27) | copy-start | bytes 1540
  7.2 156.1 %all-gather.15.cloned.1.call-start = ((), (), s32[]{:S(2)}) async-start(), calls=%async_computation.13 | async-start | bytes 1081344 | tf_op jit(solution)/shard_map/all_gather | solution.py:49
  7.9 329.5 %reduce-scatter.12.cloned.1.call-start = ((), (), s32[]{:S(2)}) async-start(), calls=%async_computation.5 | async-start | bytes 2162688 | tf_op jit(solution)/shard_map/reduce_scatter | solution.py:53
  104.5 58.7 %copy-start.7 = (f32[1,2,64,2048]{3,2,1,0:T(8,128)S(1)}, f32[1,2,64,2048]{3,2,1,0:T(8,128)}, u32[]{:S(2)}) copy-start(f32[1,2,64,2048]{3,2,1,0:T(8,128)} %param.21) | copy-start | bytes 3145732
  163.2 4.3 copy-start.4
  172.0 1.6 copy-start.12
  173.6 401.1 %reduce-scatter.16.cloned.1.call-start = ((), (), s32[]{:S(2)}) async-start(), calls=%async_computation.14 | async-start | bytes 1081344
  338.3 70.6 %collective-permute-start = (f32[128,128]{0,1:T(8,128)S(1)}, f32[128,128]{0,1:T(8,128)S(1)}, u32[]{:S(2)}, u32[]{:S(2)}) collective-permute-start(f32[128,128]{0,1:T(8,128)S(1)} %sub.65), channel_id=1, source_target_pairs={{0,32},{32,0},{64,96},{96,64},{1,33},{33,1},{65,97},{97,65},{2,34}... | collective-permute-start | bytes 196616 | tf_op jit(solution)/shard_map/ppermute | solution.py:10
  417.2 336.1 %reduce-scatter.14.cloned.1.call-start = ((), (), s32[]{:S(2)}) async-start(), calls=%async_computation.6 | async-start | bytes 4325376 | tf_op jit(solution)/shard_map/reduce_scatter | solution.py:53
  574.7 6.1 copy-start.2
  574.7 6.1 copy-start.10
  588.0 165.7 %copy-start.11 = (f32[256,128]{1,0:T(8,128)S(1)}, f32[256,128]{1,0:T(8,128)}, u32[]{:S(2)}) copy-start(f32[256,128]{1,0:T(8,128)} %param.20) | copy-start | bytes 393220
  588.0 204.2 %all-reduce.3.cloned.1.call-start = ((), (), s32[]{:S(2)}) async-start(), calls=%async_computation.7 | async-start | bytes 262144 | tf_op jit(solution)/shard_map/psum | solution.py:66
  753.3 211.5 %reduce-scatter.18.cloned.1.call-start = ((), (), s32[]{:S(2)}) async-start(), calls=%async_computation.15 | async-start | bytes 1081344 | tf_op jit(solution)/shard_map/reduce_scatter | solution.py:53
  803.9 309.5 %all-gather.7.cloned.1.call-start = ((), (), s32[]{:S(2)}) async-start(), calls=%async_computation.8 | async-start | bytes 1081344 | tf_op jit(solution)/shard_map/all_gather | solution.py:49
  964.8 197.4 %all-reduce.5.cloned.1.call-start = ((), (), s32[]{:S(2)}) async-start(), calls=%async_computation.9 | async-start | bytes 262144 | tf_op jit(solution)/shard_map/psum | solution.py:66
  1121.7 199.5 %all-gather.9.cloned.1.call-start = ((), (), s32[]{:S(2)}) async-start(), calls=%async_computation.10 | async-start | bytes 4325376 | tf_op jit(solution)/shard_map/all_gather | solution.py:49
  1162.2 328.1 %all-gather.11.cloned.1.call-start = ((), (), s32[]{:S(2)}) async-start(), calls=%async_computation.11 | async-start | bytes 1081344 | tf_op jit(solution)/shard_map/all_gather | solution.py:49
  1321.1 10.3 copy-start.3
  1321.1 10.4 copy-start.5
  1339.4 285.2 %all-gather.13.cloned.1.call-start = ((), (), s32[]{:S(2)}) async-start(), calls=%async_computation.12 | async-start | bytes 2162688 | tf_op jit(solution)/shard_map/all_gather | solution.py:49
  1497.0 1.3 collective-permute-start.1
  1499.0 299.6 %reduce-scatter.20.cloned.1.call-start = ((), (), s32[]{:S(2)}) async-start(), calls=%async_computation.16 | async-start | bytes 1081344
  1624.6 5.8 copy-start.6
  1635.2 165.0 %copy-start.1 = (s32[2,64]{1,0:T(2,128)S(1)}, s32[2,64]{1,0:T(2,128)}, u32[]{:S(2)}) copy-start(s32[2,64]{1,0:T(2,128)} %param.27) | copy-start | bytes 1540
  1636.3 1.6 copy-start.9
  1636.3 2.3 copy-start.8
Sparse Core Ops, SparseCore 0:
  9.7 153.5 all-gather.14
  173.7 163.6 reduce-scatter.11
  417.3 157.3 reduce-scatter.15
  588.2 165.0 reduce-scatter.13
  755.6 36.6 all-reduce.2
  804.0 160.7 reduce-scatter.17
  966.4 146.9 all-gather.6
  1121.8 40.3 all-reduce.4
  1163.9 157.1 all-gather.8
  1339.5 150.7 all-gather.10
  1499.1 125.4 all-gather.12
  1638.0 160.5 reduce-scatter.19
where the time goes:
time: 1820 us; the launch traced here: 1810 us
  waiting for transfers between devices  1440 us (79%)
  other arithmetic  140 us (8%)
  local copies, waits for them, and re-layouts  133 us (7%)
  matrix products  74.3 us (4%)
    all_gather x5, waiting for transfers between devices, gather_rows(): lax.all_gather(local_rows, 'front', axis=0, tiled=True)  638 us
    reduce_scatter x3, waiting for transfers between devices, scatter_rows(): lax.psum_scatter(term(jnp.int32(0), rows_each * lax.axis_size('front')),...  445 us
    unnamed x14, waiting for transfers between devices  280 us
    gather x2, local copies, waits for them, and re-layouts, pick_rows(): return jnp.take(matrix, sources, axis=1)  90.1 us
    psum x2, waiting for transfers between devices, group_total(): return lax.psum(values, 'leaf')  78.9 us
    and x2, other arithmetic, pick_rows(): return jnp.take(matrix, sources, axis=1)  59.5 us
    select_n x2, other arithmetic, pick_rows(): return jnp.take(matrix, sources, axis=1)  45.9 us
  transfers between devices with their start and end apart: 14, of which 13 were waited for; matrix products, arithmetic and copies ran while one was open for 14% of the time, Pallas kernels for 0%

commit v1 on v0

--- a/solution.py
+++ b/solution.py
@@ -46,7 +46,13 @@
 
 
 def gather_rows(local_rows, update, initial):
-    return update(initial, lax.all_gather(local_rows, "front", axis=0, tiled=True), jnp.int32(0))
+
+    def _replace_zones(view, where_dim):
+        val2 = jnp.stack([view for _ in range(lax.axis_size("front"))], axis=0)
+        local_out = lax.all_to_all(val2, "front", 0, 0)
+        return jnp.concatenate(local_out, where_dim)
+
+    return update(initial, _replace_zones(local_rows, 0), jnp.int32(0))
 
 
 def scatter_rows(term, rows_each):

time: 1820 us -> 1300 us (0.71)
  waiting for transfers between devices: 1440 us -> 802 us
  blocking collectives: 0 us -> 128 us
    all_gather x5 -> x0, waiting for transfers between devices: 638 us -> none  [gather_rows(): lax.all_gather(local_rows, 'front', axis=0, tiled=True)]
    all_to_all x0 -> x4, blocking collectives: none -> 128 us  [_replace_zones(): local_out = lax.all_to_all(val2, 'front', 0, 0)]
    unnamed x14 -> x9, waiting for transfers between devices: 280 us -> 278 us
  transfers between devices with their start and end apart: 14 -> 10, of which waited for: 13 -> 8; matrix products, arithmetic and copies ran while one was open for 14% -> 20% of each run, Pallas kernels for 0% -> 0%
where the time goes in v1:
time: 1300 us; the launch traced here: 1290 us
  waiting for transfers between devices  802 us (62%)
  other arithmetic  137 us (11%)
  local copies, waits for them, and re-layouts  134 us (10%)
  blocking collectives  128 us (10%)
  matrix products  63.6 us (5%)
  between operations  15.1 us (1%)
    reduce_scatter x3, waiting for transfers between devices, scatter_rows(): lax.psum_scatter(term(jnp.int32(0), rows_each * lax.axis_size('front')),...  447 us
    unnamed x9, waiting for transfers between devices  278 us
    all_to_all x4, blocking collectives, _replace_zones(): local_out = lax.all_to_all(val2, 'front', 0, 0)  128 us
    gather x2, local copies, waits for them, and re-layouts, pick_rows(): return jnp.take(matrix, sources, axis=1)  90.6 us
    psum x2, waiting for transfers between devices, group_total(): return lax.psum(values, 'leaf')  75.6 us
    and x2, other arithmetic, pick_rows(): return jnp.take(matrix, sources, axis=1)  59.9 us
    select_n x2, other arithmetic, pick_rows(): return jnp.take(matrix, sources, axis=1)  45.9 us
  transfers between devices with their start and end apart: 10, of which 8 were waited for; matrix products, arithmetic and copies ran while one was open for 20% of the time, Pallas kernels for 0%

profile of v1, /device:TPU:0, one launch (start us, length us, event | category | flops | bytes accessed | tf_op | source)
XLA Modules:
  0.0 1290.3 jit_solution(12815596713042956888)
XLA Ops:
  7.2 2.1 stack.10
  9.3 9.3 all-to-all-start
  18.6 2.3 sort.34
  22.3 20.0 %broadcast_clamp_fusion.1 = s32[4096]{0:T(1024)S(1)} fusion(s32[]{:T(128)} %bitcast.36, s32[]{:T(128)} %bitcast.35, s32[]{:T(128)} %bitcast.34, s32[]{:T(128)} %bitcast.33, s32[]{:T(128)} %bitcast.32, s32[]{:T(128)} %bitcast.31, s32[]{:T(128)} %bitcast.30, s32[]{:T(128)} %bitcast.29, s32[]{:T(128)} %bitcast.28, s32[]{:T(128)} %bitcast.27, s32[]{:T(128)} %bitcast.26, ...), kind=kLoop, calls=%fused_computation.209 | loop fusion | flops 356352 | bytes 16512 | tf_op gather
  42.3 20.0 %compare_and_fusion.1 = pred[4096]{0:T(1024)(128)(4,1)S(1)} fusion(s32[]{:T(128)} %bitcast.36, s32[]{:T(128)} %bitcast.35, s32[]{:T(128)} %bitcast.34, s32[]{:T(128)} %bitcast.33, s32[]{:T(128)} %bitcast.32, s32[]{:T(128)} %bitcast.31, s32[]{:T(128)} %bitcast.30, s32[]{:T(128)} %bitcast.29, s32[]{:T(128)} %bitcast.28, s32[]{:T(128)} %bitcast.27, ...), kind=kLoop, calls=%fused_computation.208 | loop fusion | flops 364544 | bytes 4224 | tf_op jit(solution)/shard_map/jit(_take)/and | solution.py:45
  62.3 4.4 copy.40
  66.7 30.8 %gather_fusion = f32[4096,2,64]{2,1,0:T(2,128)} fusion(f32[2,4096,64]{2,0,1:T(2,128)} %bitcast.210, s32[4096]{0:T(1024)S(1)} %broadcast_clamp_fusion.1), kind=kCustom, calls=%fused_computation.clone | custom fusion | bytes 4210688 | tf_op jit(solution)/shard_map/jit(_take)/gather | solution.py:45
  97.5 16.3 %select_bitcast_fusion.1 = f32[2,4096,64]{2,0,1:T(2,128)S(1)} fusion(f32[4096,2,64]{2,1,0:T(2,128)} %gather_fusion, pred[4096]{0:T(1024)(128)(4,1)S(1)} %compare_and_fusion.1), kind=kLoop, calls=%fused_computation.4 | loop fusion | flops 524288 | bytes 4198400 | tf_op jit(solution)/shard_map/jit(_take)/select_n | solution.py:45
  113.8 4.1 fusion.156
  117.9 1.9 fusion.25
  119.9 1.8 fusion.28
  121.9 2.1 fusion.163
  124.0 2.1 fusion.164
  126.4 1.5 pad_maximum_fusion.1
  128.1 2.0 sort.35
  133.4 39.9 %compare_and_fusion = (pred[8192]{0:T(1024)(128)(4,1)S(1)}, s32[8192]{0:T(1024)S(1)}) fusion(s32[]{:T(128)} %bitcast.110, s32[]{:T(128)} %bitcast.109, s32[]{:T(128)} %bitcast.108, s32[]{:T(128)} %bitcast.107, s32[]{:T(128)} %bitcast.106, s32[]{:T(128)} %bitcast.105, s32[]{:T(128)} %bitcast.104, s32[]{:T(128)} %bitcast.103, s32[]{:T(128)} %bitcast.102, ...), kind=kLoop, calls=%fused_computation.164 | loop fusion | flops 1253376 | bytes 41216 | tf_op jit(solution)/shard_map/jit(_take)/and | solution.py:45
  173.3 119.5 %reduce-scatter.12.cloned.1.call-done = f32[128,128]{0,1:T(8,128)} async-done(((f32[4096,128]{0,1:T(8,128)}), f32[128,128]{0,1:T(8,128)}) %reduce-scatter.12.cloned.1.call-update) | async-done | bytes 65552 | tf_op jit(solution)/shard_map/reduce_scatter | solution.py:59
  293.9 10.8 copy.42
  304.7 59.9 %gather_fusion.1 = f32[8192,2,64]{2,1,0:T(2,128)} fusion(f32[2,8192,64]{2,0,1:T(2,128)} %bitcast.203, s32[8192]{0:T(1024)S(1)} %broadcast_clamp_fusion), kind=kCustom, calls=%fused_computation.1.clone | custom fusion | bytes 8421376 | tf_op jit(solution)/shard_map/jit(_take)/gather | solution.py:45
  364.6 2.2 convolution_bitcast_fusion.3
  366.8 2.2 convolution_bitcast_fusion.2
  369.3 1.4 copy.51
  370.8 29.5 %select_bitcast_fusion = f32[2,8192,64]{2,0,1:T(2,128)S(1)} fusion(f32[8192,2,64]{2,1,0:T(2,128)} %gather_fusion.1, pred[8192]{0:T(1024)(128)(4,1)S(1)} %get-tuple-element.20), kind=kLoop, calls=%fused_computation.2 | loop fusion | flops 1048576 | bytes 8396800 | tf_op jit(solution)/shard_map/jit(_take)/select_n | solution.py:45
  400.3 7.7 fusion.155
  408.1 120.1 %reduce-scatter.16.cloned.1.call-done = f32[64,128]{1,0:T(8,128)} async-done(((f32[2048,128]{1,0:T(8,128)}), f32[64,128]{1,0:T(8,128)}) %reduce-scatter.16.cloned.1.call-update) | async-done | bytes 32784
  528.2 6.0 fusion.165
  534.3 4.4 fusion.166
  539.2 2.3 pad_maximum_fusion
  541.6 165.4 %reduce-scatter.14.cloned.1.call-done = f32[256,128]{0,1:T(8,128)} async-done(((f32[8192,128]{0,1:T(8,128)}), f32[256,128]{0,1:T(8,128)}) %reduce-scatter.14.cloned.1.call-update) | async-done | bytes 131088 | tf_op jit(solution)/shard_map/reduce_scatter | solution.py:59
  707.5 37.7 %all-reduce.3.cloned.1.call-done = f32[256,128]{0,1:T(8,128)} async-done(((f32[256,128]{0,1:T(8,128)}), f32[256,128]{0,1:T(8,128)}) %all-reduce.3.cloned.1.call-update) | async-done | bytes 131088 | tf_op jit(solution)/shard_map/psum | solution.py:72
  745.3 3.9 convolution_bitcast_fusion.5
  749.1 3.9 convolution_bitcast_fusion.4
  753.3 1.4 copy.53
  754.8 162.3 %reduce-scatter.18.cloned.1.call-done = f32[64,128]{1,0:T(8,128)} async-done(((f32[2048,128]{1,0:T(8,128)}), f32[64,128]{1,0:T(8,128)}) %reduce-scatter.18.cloned.1.call-update) | async-done | bytes 32784 | tf_op jit(solution)/shard_map/reduce_scatter | solution.py:59
  918.1 16.1 %all_to_all.25 = f32[32,64,128]{2,1,0:T(8,128)S(1)} all-to-all(f32[32,64,128]{2,1,0:T(8,128)S(1)} %stack.11), channel_id=1, replica_groups=mesh['leaf'=4,'front'=32] {'front'}, dimensions={0} | all-to-all | bytes 2097152 | tf_op jit(solution)/shard_map/all_to_all | solution.py:52
  934.2 3.4 fusion.10
  937.6 1.9 fusion.13
  940.3 37.8 %all-reduce.5.cloned.1.call-done = f32[256,128]{0,1:T(8,128)} async-done(((f32[256,128]{0,1:T(8,128)}), f32[256,128]{0,1:T(8,128)}) %all-reduce.5.cloned.1.call-update) | async-done | bytes 131088 | tf_op jit(solution)/shard_map/psum | solution.py:72
  979.6 58.4 %all_to_all.26 = f32[32,256,128]{2,1,0:T(8,128)S(1)} all-to-all(f32[32,256,128]{2,1,0:T(8,128)S(1)} %stack.12), channel_id=1, replica_groups=mesh['leaf'=4,'front'=32] {'front'}, dimensions={0} | all-to-all | bytes 8388608 | tf_op jit(solution)/shard_map/all_to_all | solution.py:52
  1038.0 7.1 fusion.167
  1045.2 7.3 fusion.168
  1052.8 20.6 %all_to_all.27 = f32[32,64,128]{2,1,0:T(8,128)S(1)} all-to-all(f32[32,64,128]{2,1,0:T(8,128)S(1)} %stack.13), channel_id=1, replica_groups=mesh['leaf'=4,'front'=32] {'front'}, dimensions={0} | all-to-all | bytes 2097152 | tf_op jit(solution)/shard_map/all_to_all | solution.py:52
  1073.5 1.9 convolution_bitcast_fusion.6
  1075.3 1.9 convolution_bitcast_fusion.7
  1078.9 32.7 %all_to_all.28 = f32[32,128,128]{2,1,0:T(8,128)S(1)} all-to-all(f32[32,128,128]{2,1,0:T(8,128)S(1)} %stack.14), channel_id=1, replica_groups=mesh['leaf'=4,'front'=32] {'front'}, dimensions={0} | all-to-all | bytes 4194304 | tf_op jit(solution)/shard_map/all_to_all | solution.py:52
  1111.6 3.6 fusion.169
  1115.1 3.7 fusion.170
  1123.5 158.1 %reduce-scatter.20.cloned.1.call-done = f32[64,128]{1,0:T(8,128)} async-done(((f32[2048,128]{1,0:T(8,128)}), f32[64,128]{1,0:T(8,128)}) %reduce-scatter.20.cloned.1.call-update) | async-done | bytes 32784
  (95 shorter events, 19.4 us)
Async XLA Ops:
  7.2 120.9 %copy-start = (s32[2,64]{1,0:T(2,128)S(1)}, s32[2,64]{1,0:T(2,128)}, u32[]{:S(2)}) copy-start(s32[2,64]{1,0:T(2,128)} %param.27) | copy-start | bytes 1540
  7.2 55.1 %copy-start.10 = (f32[1,2,4096,64]{2,3,1,0:T(8,128)S(1)}, f32[1,2,4096,64]{2,3,1,0:T(8,128)}, u32[]{:S(2)}) copy-start(f32[1,2,4096,64]{2,3,1,0:T(8,128)} %param.22) | copy-start | bytes 6291460
  9.3 108.7 %all-to-all-start = ((f32[32,64,128]{2,1,0:T(8,128)}), f32[32,64,128]{2,1,0:T(8,128)S(1)}, u32[]{:S(2)}, u32[]{:S(2)}) async-start(f32[32,64,128]{2,1,0:T(8,128)} %stack.10), calls=%async_computation | async-start | bytes 2097152 | tf_op jit(solution)/shard_map/all_to_all | solution.py:52
  18.5 274.3 %reduce-scatter.12.cloned.1.call-start = ((), (), s32[]{:S(2)}) async-start(), calls=%async_computation.10 | async-start | bytes 2162688 | tf_op jit(solution)/shard_map/reduce_scatter | solution.py:59
  117.9 3.9 copy-start.5
  126.4 1.6 copy-start.14
  127.9 400.3 %reduce-scatter.16.cloned.1.call-start = ((), (), s32[]{:S(2)}) async-start(), calls=%async_computation.14 | async-start | bytes 1081344
  293.7 70.9 %collective-permute-start = (f32[128,128]{0,1:T(8,128)S(1)}, f32[128,128]{0,1:T(8,128)S(1)}, u32[]{:S(2)}, u32[]{:S(2)}) collective-permute-start(f32[128,128]{0,1:T(8,128)S(1)} %sub.65), channel_id=1, source_target_pairs={{0,32},{32,0},{64,96},{96,64},{1,33},{33,1},{65,97},{97,65},{2,34}... | collective-permute-start | bytes 196616 | tf_op jit(solution)/shard_map/ppermute | solution.py:10
  370.7 336.2 %reduce-scatter.14.cloned.1.call-start = ((), (), s32[]{:S(2)}) async-start(), calls=%async_computation.11 | async-start | bytes 4325376 | tf_op jit(solution)/shard_map/reduce_scatter | solution.py:59
  528.2 6.1 copy-start.2
  528.2 6.1 copy-start.12
  541.5 165.9 %copy-start.13 = (f32[256,128]{1,0:T(8,128)S(1)}, f32[256,128]{1,0:T(8,128)}, u32[]{:S(2)}) copy-start(f32[256,128]{1,0:T(8,128)} %param.20) | copy-start | bytes 393220
  541.5 203.7 %all-reduce.3.cloned.1.call-start = ((), (), s32[]{:S(2)}) async-start(), calls=%async_computation.12 | async-start | bytes 262144 | tf_op jit(solution)/shard_map/psum | solution.py:72
  706.9 210.1 %reduce-scatter.18.cloned.1.call-start = ((), (), s32[]{:S(2)}) async-start(), calls=%async_computation.15 | async-start | bytes 1081344 | tf_op jit(solution)/shard_map/reduce_scatter | solution.py:59
  754.7 223.4 %all-reduce.5.cloned.1.call-start = ((), (), s32[]{:S(2)}) async-start(), calls=%async_computation.13 | async-start | bytes 262144 | tf_op jit(solution)/shard_map/psum | solution.py:72
  917.1 20.5 %copy-start.7 = (f32[2,2048,256]{2,1,0:T(8,128)S(1)}, f32[2,2048,256]{2,1,0:T(8,128)}, u32[]{:S(2)}) copy-start(f32[2,2048,256]{2,1,0:T(8,128)} %param.25) | copy-start | bytes 12582916
  940.2 341.3 %reduce-scatter.20.cloned.1.call-start = ((), (), s32[]{:S(2)}) async-start(), calls=%async_computation.16 | async-start | bytes 1081344
  979.1 58.9 %copy-start.11 = (f32[256,128]{1,0:T(8,128)}, f32[256,128]{1,0:T(8,128)S(1)}, u32[]{:S(2)}) copy-start(f32[256,128]{1,0:T(8,128)S(1)} %copy.45) | copy-start | bytes 393220
  979.6 58.4 %copy-start.4 = (f32[1,8192,64]{2,0,1:T(1,128)S(1)}, f32[1,8192,64]{2,0,1:T(1,128)}, u32[]{:S(2)}) copy-start(f32[1,8192,64]{2,0,1:T(1,128)} %get-tuple-element.24) | copy-start | bytes 6291460
  1038.0 7.1 copy-start.3
  1045.2 28.3 %copy-start.8 = (f32[1,2,2048,128]{3,2,1,0:T(8,128)S(1)}, f32[1,2,2048,128]{3,2,1,0:T(8,128)}, u32[]{:S(2)}) copy-start(f32[1,2,2048,128]{3,2,1,0:T(8,128)} %param.23) | copy-start | bytes 6291460
  1077.2 1.3 collective-permute-start.1
  1078.7 32.9 %copy-start.6 = (f32[1,4096,64]{2,0,1:T(1,128)S(1)}, f32[1,4096,64]{2,0,1:T(1,128)}, u32[]{:S(2)}) copy-start(f32[1,4096,64]{2,0,1:T(1,128)} %get-tuple-element.28) | copy-start | bytes 3145732
  1111.6 7.3 copy-start.9
  1120.0 163.1 %copy-start.1 = (s32[2,64]{1,0:T(2,128)S(1)}, s32[2,64]{1,0:T(2,128)}, u32[]{:S(2)}) copy-start(s32[2,64]{1,0:T(2,128)} %param.27) | copy-start | bytes 1540
Sparse Core Ops, SparseCore 0:
  128.0 164.7 reduce-scatter.11
  370.8 157.3 reduce-scatter.15
  541.6 165.2 reduce-scatter.13
  709.2 35.9 all-reduce.2
  754.8 162.2 reduce-scatter.17
  940.3 37.7 all-reduce.4
  1122.8 158.6 reduce-scatter.19
